TPU v7x, 512 devices: a whole 4x8x8 slice. The times are simulated.
512 devices in a mesh: mode: 2 (over core), oth: 256 (over z, y, x).
Axes of the slice: x: 4, y: 8, z: 8, core: 2. Of those that a mesh axis runs over, the one named last changes fastest.
Arguments:
- tensor: float32 [512, 4, 262144], P('mode', None, 'oth'), may hold values from -20 to 20
- start_basis: float32 [512, 128], replicated, may hold values from -6 to 6
Outputs:
- core_slab: float32 [128, 4, 262144], P('mode', None, 'oth')
- triangle: float32 [512, 512], replicated
All inputs are finite; a program needn't handle non-finite values.
Results may differ from a plain program's by a relative error of at most 0.0003.
Values sent between devices are 32-bit elements; how exact they have to be, the bound alone decides.
A program may use at most 64 MiB of HBM per device.

v0:
```python
import jax
import jax.numpy as jnp
from jax import lax
from jax.sharding import PartitionSpec as P

ITERS = 3


def subspace(triangle, start_basis):
    basis = start_basis
    for sweep in range(ITERS):
        reduced = jnp.dot(
            triangle.T, basis, precision=lax.Precision.HIGHEST, preferred_element_type=jnp.float32
        )
        images = jnp.dot(
            triangle, reduced, precision=lax.Precision.HIGHEST, preferred_element_type=jnp.float32
        )
        gram_small = jnp.dot(
            images.T, images, precision=lax.Precision.HIGHEST, preferred_element_type=jnp.float32
        )
        factor_lower = jnp.linalg.cholesky(gram_small)
        basis = lax.linalg.triangular_solve(
            factor_lower, images, left_side=False, lower=True, transpose_a=True
        )
    return basis


def local(tensor, start_basis):
    rows_local, components, cell_count = tensor.shape
    group_size = lax.axis_size("mode")
    column_total = components * cell_count * lax.axis_size("oth")
    fibers_full = lax.all_to_all(tensor, "mode", split_axis=2, concat_axis=0, tiled=True)
    full_rows = fibers_full.shape[0]
    unfolded = fibers_full.reshape(full_rows, -1)
    covar_part = (
        jnp.dot(
            unfolded,
            unfolded.T,
            precision=lax.Precision.HIGHEST,
            preferred_element_type=jnp.float32,
        )
        / column_total
    )
    flat_part = covar_part.reshape(full_rows * full_rows)
    summed_piece = lax.psum_scatter(flat_part, ("mode", "oth"), scatter_dimension=0, tiled=True)
    summed_covar = lax.all_gather(summed_piece, ("mode", "oth"), axis=0, tiled=True).reshape(
        full_rows, full_rows
    )
    triangle = jnp.linalg.cholesky(summed_covar)
    basis = subspace(triangle, start_basis)
    rank_total = basis.shape[1]
    mode_index = lax.axis_index("mode")
    own_rows = lax.dynamic_slice_in_dim(basis, mode_index * rows_local, rows_local, 0)
    local_unfolded = tensor.reshape(rows_local, -1)
    product = lax.dot_general(
        own_rows,
        local_unfolded,
        (((0,), (0,)), ((), ())),
        precision=lax.Precision.HIGHEST,
        preferred_element_type=jnp.float32,
    )
    core_slab = lax.psum_scatter(
        product.reshape(lax.axis_size("mode") * (rank_total // group_size), components, cell_count),
        "mode",
        scatter_dimension=0,
        tiled=True,
    )
    return (core_slab, triangle)


def solution(mesh):
    return jax.shard_map(
        local,
        mesh=mesh,
        in_specs=(P("mode", None, "oth"), P()),
        out_specs=(P("mode", None, "oth"), P()),
        check_vma=False,
    )
```

profile of v0, /device:TPU:1, one launch (start us, length us, event | category | flops | bytes accessed | tf_op | source)
XLA Modules:
  0.0 643.0 jit_solution(9546581247558276727)
XLA Ops:
  7.2 6.5 %copy.27 = f32[256,4,1024]{0,1,2:T(4,128)} copy(f32[256,4,1024]{2,1,0:T(4,128)} %param.5) | data formatting | bytes 8388608 | tf_op args[0]
  13.8 18.3 %all_to_all.15 = f32[256,4,1024]{0,1,2:T(4,128)} all-to-all(f32[256,4,1024]{0,1,2:T(4,128)} %copy.27), channel_id=1, replica_groups=mesh['mode'=2,'oth'=256] {'mode'}, dimensions={2} | all-to-all | bytes 8388608 | tf_op jit(solution)/shard_map/all_to_all | solution.py:32
  32.1 7.3 %copy.28 = f32[256,4,2,512]{3,1,0,2:T(4,128)} copy(f32[256,4,2,512]{0,1,3,2:T(4,128)} %bitcast.103) | data formatting | bytes 8388608 | tf_op jit(solution)/shard_map/all_to_all | solution.py:32
  43.5 6.9 %fusion = f32[64,4,8,128]{3,2,1,0:T(8,128)S(1)} fusion(f32[512,2048]{1,0:T(8,128)S(1)} %bitcast.100), kind=kOutput, calls=%fused_computation.1 | convolution fusion | flops 6442713088 | bytes 5242880 | tf_op jit(solution)/shard_map/dot_general | solution.py:36
  51.8 274.5 %all-reduce.4.cloned.1.call-done = f32[262144]{0:T(1024)} async-done(((f32[262144]{0:T(1024)}), f32[262144]{0:T(1024)}) %all-reduce.4.cloned.1.call-update) | async-done | bytes 1048592
  327.7 11.7 %reduce-scatter.2.cloned.1.call-start = ((), (), s32[]{:S(2)}) async-start(), calls=%async_computation.2 | async-start | bytes 3145728 | tf_op jit(solution)/shard_map/reduce_scatter | solution.py:62
  339.4 8.0 %copy.39 = f32[32,8,4,1024]{3,1,2,0:T(8,128)} copy(f32[32,8,4,1024]{3,2,1,0:T(4,128)} %bitcast.101) | data formatting | bytes 8388608
  347.3 5.6 copy.34
  352.9 86.7 %all-gather.3.cloned.1.call-done = f32[512,1,512]{2,1,0:T(1,128)} async-done(((f32[1,1,512]{2,1,0:T(1,128)}), f32[512,1,512]{2,1,0:T(1,128)}) %all-gather.3.cloned.1.call-update) | async-done | bytes 1048592 | tf_op jit(solution)/shard_map/all_gather | solution.py:46
  443.4 11.7 %cholesky.120 = f32[128,128]{1,0:T(8,128)S(1)} custom-call(f32[128,128]{1,0:T(8,128)S(1)} %cholesky.356), custom_call_target="Cholesky" | custom-call | tf_op jit(solution)/shard_map/jit(cholesky)/cholesky | solution.py:49
  455.2 9.8 %custom-call.32 = f32[1,128,128]{1,2,0:T(8,128)S(1)} custom-call(f32[1,128,128]{2,1,0:T(8,128)S(1)} %get-tuple-element.21), custom_call_target="InvertDiagBlocksLowerTriangular" | custom-call | tf_op jit(solution)/shard_map/jit(cholesky)/cholesky | solution.py:49
  465.8 11.7 %cholesky.244 = f32[128,128]{1,0:T(8,128)S(1)} custom-call(f32[128,128]{1,0:T(8,128)S(1)} %cholesky.360), custom_call_target="Cholesky" | custom-call | tf_op jit(solution)/shard_map/jit(cholesky)/cholesky | solution.py:49
  477.5 10.2 %custom-call.33 = f32[1,128,128]{1,2,0:T(8,128)S(1)} custom-call(f32[1,128,128]{2,1,0:T(8,128)S(1)} %get-tuple-element.18), custom_call_target="InvertDiagBlocksLowerTriangular" | custom-call | tf_op jit(solution)/shard_map/jit(cholesky)/cholesky | solution.py:49
  488.4 11.7 %cholesky.265 = f32[128,128]{1,0:T(8,128)S(1)} custom-call(f32[128,128]{1,0:T(8,128)S(1)} %cholesky.365), custom_call_target="Cholesky" | custom-call | tf_op jit(solution)/shard_map/jit(cholesky)/cholesky | solution.py:49
  500.8 9.8 %custom-call.34 = f32[1,128,128]{1,2,0:T(8,128)S(1)} custom-call(f32[1,128,128]{2,1,0:T(8,128)S(1)} %get-tuple-element.15), custom_call_target="InvertDiagBlocksLowerTriangular" | custom-call | tf_op jit(solution)/shard_map/jit(cholesky)/cholesky | solution.py:49
  511.2 11.7 %cholesky.282 = f32[128,128]{1,0:T(8,128)S(1)} custom-call(f32[128,128]{1,0:T(8,128)S(1)} %convolution_subtract_fusion.2), custom_call_target="Cholesky" | custom-call | tf_op jit(solution)/shard_map/jit(cholesky)/cholesky | solution.py:49
  530.6 11.7 %cholesky.325 = f32[128,128]{1,0:T(8,128)S(1)} custom-call(f32[128,128]{1,0:T(8,128)S(1)} %fusion.21), custom_call_target="Cholesky" | custom-call | tf_op jit(solution)/shard_map/jit(cholesky)/cholesky | solution.py:21
  543.7 9.8 %custom-call.37 = f32[1,128,128]{1,2,0:T(8,128)S(1)} custom-call(f32[1,128,128]{2,1,0:T(8,128)S(1)} %fusion.11), custom_call_target="InvertDiagBlocksLowerTriangular" | custom-call | tf_op jit(solution)/shard_map/triangular_solve/custom-call.8 | solution.py:22
  557.7 11.7 %cholesky.336 = f32[128,128]{1,0:T(8,128)S(1)} custom-call(f32[128,128]{1,0:T(8,128)S(1)} %fusion.19), custom_call_target="Cholesky" | custom-call | tf_op jit(solution)/shard_map/jit(cholesky)/cholesky | solution.py:21
  570.7 9.8 %custom-call.38 = f32[1,128,128]{1,2,0:T(8,128)S(1)} custom-call(f32[1,128,128]{2,1,0:T(8,128)S(1)} %fusion.12), custom_call_target="InvertDiagBlocksLowerTriangular" | custom-call | tf_op jit(solution)/shard_map/triangular_solve/custom-call.8 | solution.py:22
  584.5 12.0 %cholesky.347 = f32[128,128]{1,0:T(8,128)S(1)} custom-call(f32[128,128]{1,0:T(8,128)S(1)} %fusion.17), custom_call_target="Cholesky" | custom-call | tf_op jit(solution)/shard_map/jit(cholesky)/cholesky | solution.py:21
  597.8 9.8 %custom-call.39 = f32[1,128,128]{1,2,0:T(8,128)S(1)} custom-call(f32[1,128,128]{2,1,0:T(8,128)S(1)} %fusion.13), custom_call_target="InvertDiagBlocksLowerTriangular" | custom-call | tf_op jit(solution)/shard_map/triangular_solve/custom-call.8 | solution.py:22
  608.0 7.8 %fusion.8 = f32[128,4,1024]{2,0,1:T(8,128)} fusion(f32[4,1024,256]{2,1,0:T(8,128)} %bitcast.102, f32[512,128]{0,1:T(8,128)S(1)} %convolution_bitcast_fusion, s32[]{:T(128)S(6)} %select_n.11), kind=kOutput, calls=%fused_computation.20 | convolution fusion | flops 1610612736 | bytes 6422532 | tf_op jit(solution)/shard_map/dot_general | solution.py:55
  615.8 17.3 %reduce-scatter.2.cloned.1.call-done = f32[64,4,1024]{2,0,1:T(8,128)} async-done(((f32[128,4,1024]{2,0,1:T(8,128)}), f32[64,4,1024]{2,0,1:T(8,128)}) %reduce-scatter.2.cloned.1.call-update) | async-done | bytes 1048592 | tf_op jit(solution)/shard_map/reduce_scatter | solution.py:62
  (60 shorter events, 33.8 us)
Async XLA Ops:
  7.2 519.8 %copy-start = (f32[512,128]{1,0:T(8,128)S(1)}, f32[512,128]{1,0:T(8,128)}, u32[]{:S(2)}) copy-start(f32[512,128]{1,0:T(8,128)} %param.6) | copy-start | bytes 786436
  7.2 319.1 %all-reduce.4.cloned.1.call-start = ((), (), s32[]{:S(2)}) async-start(), calls=%async_computation.4 | async-start | bytes 2097152
  51.7 387.9 %all-gather.3.cloned.1.call-start = ((), (), s32[]{:S(2)}) async-start(), calls=%async_computation.3 | async-start | bytes 1050624 | tf_op jit(solution)/shard_map/all_gather | solution.py:46
  327.7 305.5 %reduce-scatter.2.cloned.1.call-start = ((), (), s32[]{:S(2)}) async-start(), calls=%async_computation.2 | async-start | bytes 3145728 | tf_op jit(solution)/shard_map/reduce_scatter | solution.py:62
  526.9 55.8 %copy-start.1 = (f32[512,512]{1,0:T(8,128)}, f32[512,512]{1,0:T(8,128)S(1)}, u32[]{:S(2)}) copy-start(f32[512,512]{1,0:T(8,128)S(1)} %select_select_fusion) | copy-start | bytes 3145732
Sparse Core Ops, SparseCore 0:
  51.8 274.4 all-reduce.3
  331.1 108.5 all-gather.2
  616.0 17.1 reduce-scatter.1
where the time goes:
time: 651 us; the launch traced here: 643 us
  waiting for transfers between devices  379 us (58%)
  other arithmetic  149 us (23%)
  local copies, waits for them, and re-layouts  39.7 us (6%)
  matrix products  28.3 us (4%)
  blocking collectives  18.3 us (3%)
  between operations  17 us (3%)
  starting transfers between devices  11.8 us (2%)
    unnamed x4, waiting for transfers between devices  275 us
    all_gather x1, waiting for transfers between devices, local(): lax.all_gather(summed_piece, ('mode', 'oth'), axis=0, tiled=True)  86.7 us
    another operation x14, other arithmetic, local(): triangle = jnp.linalg.cholesky(summed_covar)  78.8 us
    another operation x9, other arithmetic, subspace(): factor_lower = jnp.linalg.cholesky(gram_small)  37.4 us
    another operation x6, other arithmetic, subspace(): lax.linalg.triangular_solve(factor_lower, images, left_side=False, lower=...  31.4 us
    unnamed x10, local copies, waits for them, and re-layouts  24.1 us
    all_to_all x1, blocking collectives, local(): lax.all_to_all(tensor, 'mode', split_axis=2, concat_axis=0, tiled=True)  18.3 us
    reduce_scatter x1, waiting for transfers between devices, local(): lax.psum_scatter(product.reshape(lax.axis_size('mode') * (rank_total // g...  17.3 us
  transfers between devices with their start and end apart: 3, of which 3 were waited for; matrix products, arithmetic and copies ran while one was open for 2% of the time, Pallas kernels for 0%

commit v1 on v0

--- a/solution.py
+++ b/solution.py
@@ -1,9 +1,21 @@
+import functools
 import jax
 import jax.numpy as jnp
 from jax import lax
 from jax.sharding import PartitionSpec as P
 
 ITERS = 3
+
+
+def start_the_yards(field, at_axis):
+    local_next = lax.axis_size(("mode", "oth"))
+    y2 = jnp.stack([field] * local_next, axis=0)
+    block_now = lax.all_to_all(y2, ("mode", "oth"), 0, 0)
+    k_now = jnp.concatenate(block_now, axis=at_axis)
+    return k_now
+
+
+_balance_kinds = functools.partial(start_the_yards, at_axis=0)
 
 
 def subspace(triangle, start_basis):
@@ -43,9 +55,7 @@
     )
     flat_part = covar_part.reshape(full_rows * full_rows)
     summed_piece = lax.psum_scatter(flat_part, ("mode", "oth"), scatter_dimension=0, tiled=True)
-    summed_covar = lax.all_gather(summed_piece, ("mode", "oth"), axis=0, tiled=True).reshape(
-        full_rows, full_rows
-    )
+    summed_covar = _balance_kinds(summed_piece).reshape(full_rows, full_rows)
     triangle = jnp.linalg.cholesky(summed_covar)
     basis = subspace(triangle, start_basis)
     rank_total = basis.shape[1]

time: 651 us -> 578 us (0.89)
  waiting for transfers between devices: 379 us -> 305 us
    all_gather x1 -> x0, waiting for transfers between devices: 86.7 us -> none  [local(): lax.all_gather(summed_piece, ('mode', 'oth'), axis=0, tiled=True)]
    all_to_all x0 -> x1, waiting for transfers between devices: none -> 18.7 us  [start_the_yards(): block_now = lax.all_to_all(y2, ('mode', 'oth'), 0, 0)]
    all_to_all x0 -> x1, starting transfers between devices: none -> 12.9 us  [start_the_yards(): block_now = lax.all_to_all(y2, ('mode', 'oth'), 0, 0)]
    reduce_scatter x1, starting transfers between devices: 11.7 us -> 0.04 us  [local(): lax.psum_scatter(product.reshape(lax.axis_size('mode') * (rank_total // g...]
    unnamed x4 -> x3, waiting for transfers between devices: 275 us -> 275 us
where the time goes in v1:
time: 578 us; the launch traced here: 569 us
  waiting for transfers between devices  305 us (53%)
  other arithmetic  148 us (26%)
  local copies, waits for them, and re-layouts  39.8 us (7%)
  matrix products  28.5 us (5%)
  blocking collectives  18.3 us (3%)
  between operations  17.1 us (3%)
  starting transfers between devices  13 us (2%)
    unnamed x3, waiting for transfers between devices  275 us
    another operation x14, other arithmetic, local(): triangle = jnp.linalg.cholesky(summed_covar)  78.6 us
    another operation x9, other arithmetic, subspace(): factor_lower = jnp.linalg.cholesky(gram_small)  37.4 us
    another operation x6, other arithmetic, subspace(): lax.linalg.triangular_solve(factor_lower, images, left_side=False, lower=...  31.4 us
    unnamed x10, local copies, waits for them, and re-layouts  23.5 us
    all_to_all x1, waiting for transfers between devices, start_the_yards(): block_now = lax.all_to_all(y2, ('mode', 'oth'), 0, 0)  18.7 us
    all_to_all x1, blocking collectives, local(): lax.all_to_all(tensor, 'mode', split_axis=2, concat_axis=0, tiled=True)  18.3 us
    all_to_all x1, starting transfers between devices, start_the_yards(): block_now = lax.all_to_all(y2, ('mode', 'oth'), 0, 0)  12.9 us
  transfers between devices with their start and end apart: 3, of which 3 were waited for; matrix products, arithmetic and copies ran while one was open for 2% of the time, Pallas kernels for 0%

profile of v1, /device:TPU:1, one launch (start us, length us, event | category | flops | bytes accessed | tf_op | source)
XLA Modules:
  0.0 569.5 jit_solution(8290222718828596842)
XLA Ops:
  7.2 6.5 %copy.26 = f32[256,4,1024]{0,1,2:T(4,128)} copy(f32[256,4,1024]{2,1,0:T(4,128)} %param.5) | data formatting | bytes 8388608 | tf_op args[0]
  13.8 18.3 %all_to_all.24 = f32[256,4,1024]{0,1,2:T(4,128)} all-to-all(f32[256,4,1024]{0,1,2:T(4,128)} %copy.26), channel_id=1, replica_groups=mesh['mode'=2,'oth'=256] {'mode'}, dimensions={2} | all-to-all | bytes 8388608 | tf_op jit(solution)/shard_map/all_to_all | solution.py:44
  32.1 7.3 %copy.27 = f32[256,4,2,512]{3,1,0,2:T(4,128)} copy(f32[256,4,2,512]{0,1,3,2:T(4,128)} %bitcast.102) | data formatting | bytes 8388608 | tf_op jit(solution)/shard_map/all_to_all | solution.py:44
  43.5 6.9 %fusion = f32[64,4,8,128]{3,2,1,0:T(8,128)S(1)} fusion(f32[512,2048]{1,0:T(8,128)S(1)} %bitcast.99), kind=kOutput, calls=%fused_computation.1 | convolution fusion | flops 6442713088 | bytes 5242880 | tf_op jit(solution)/shard_map/dot_general | solution.py:48
  51.7 274.6 %all-reduce.4.cloned.1.call-done = f32[262144]{0:T(1024)} async-done(((f32[262144]{0:T(1024)}), f32[262144]{0:T(1024)}) %all-reduce.4.cloned.1.call-update) | async-done | bytes 1048592
  328.5 12.9 %all-to-all-start.1 = ((f32[512,1,512]{2,1,0:T(1,128)}), f32[512,1,512]{2,1,0:T(1,128)S(1)}, u32[]{:S(2)}, u32[]{:S(2)}) async-start(f32[512,1,512]{2,1,0:T(1,128)} %stack.2), calls=%async_computation.1 | async-start | bytes 2097152 | tf_op jit(solution)/shard_map/all_to_all | solution.py:13
  341.5 8.0 %copy.38 = f32[32,8,4,1024]{3,1,2,0:T(8,128)} copy(f32[32,8,4,1024]{3,2,1,0:T(4,128)} %bitcast.100) | data formatting | bytes 8388608
  349.4 5.6 copy.33
  355.0 18.7 %all-to-all-done.1 = f32[512,1,512]{2,1,0:T(1,128)S(1)} async-done(((f32[512,1,512]{2,1,0:T(1,128)}), f32[512,1,512]{2,1,0:T(1,128)S(1)}, u32[]{:S(2)}, u32[]{:S(2)}) %all-to-all-start.1) | async-done | bytes 1048608 | tf_op jit(solution)/shard_map/all_to_all | solution.py:13
  375.5 11.7 %cholesky.120 = f32[128,128]{1,0:T(8,128)S(1)} custom-call(f32[128,128]{1,0:T(8,128)S(1)} %cholesky.356), custom_call_target="Cholesky" | custom-call | tf_op jit(solution)/shard_map/jit(cholesky)/cholesky | solution.py:59
  387.2 9.8 %custom-call.32 = f32[1,128,128]{1,2,0:T(8,128)S(1)} custom-call(f32[1,128,128]{2,1,0:T(8,128)S(1)} %get-tuple-element.21), custom_call_target="InvertDiagBlocksLowerTriangular" | custom-call | tf_op jit(solution)/shard_map/jit(cholesky)/cholesky | solution.py:59
  397.9 11.7 %cholesky.244 = f32[128,128]{1,0:T(8,128)S(1)} custom-call(f32[128,128]{1,0:T(8,128)S(1)} %cholesky.360), custom_call_target="Cholesky" | custom-call | tf_op jit(solution)/shard_map/jit(cholesky)/cholesky | solution.py:59
  409.6 10.0 %custom-call.33 = f32[1,128,128]{1,2,0:T(8,128)S(1)} custom-call(f32[1,128,128]{2,1,0:T(8,128)S(1)} %get-tuple-element.18), custom_call_target="InvertDiagBlocksLowerTriangular" | custom-call | tf_op jit(solution)/shard_map/jit(cholesky)/cholesky | solution.py:59
  420.3 11.7 %cholesky.265 = f32[128,128]{1,0:T(8,128)S(1)} custom-call(f32[128,128]{1,0:T(8,128)S(1)} %cholesky.365), custom_call_target="Cholesky" | custom-call | tf_op jit(solution)/shard_map/jit(cholesky)/cholesky | solution.py:59
  432.7 9.8 %custom-call.34 = f32[1,128,128]{1,2,0:T(8,128)S(1)} custom-call(f32[1,128,128]{2,1,0:T(8,128)S(1)} %get-tuple-element.15), custom_call_target="InvertDiagBlocksLowerTriangular" | custom-call | tf_op jit(solution)/shard_map/jit(cholesky)/cholesky | solution.py:59
  443.1 11.7 %cholesky.282 = f32[128,128]{1,0:T(8,128)S(1)} custom-call(f32[128,128]{1,0:T(8,128)S(1)} %convolution_subtract_fusion.2), custom_call_target="Cholesky" | custom-call | tf_op jit(solution)/shard_map/jit(cholesky)/cholesky | solution.py:59
  462.8 11.7 %cholesky.325 = f32[128,128]{1,0:T(8,128)S(1)} custom-call(f32[128,128]{1,0:T(8,128)S(1)} %fusion.21), custom_call_target="Cholesky" | custom-call | tf_op jit(solution)/shard_map/jit(cholesky)/cholesky | solution.py:33
  475.8 9.8 %custom-call.37 = f32[1,128,128]{1,2,0:T(8,128)S(1)} custom-call(f32[1,128,128]{2,1,0:T(8,128)S(1)} %fusion.11), custom_call_target="InvertDiagBlocksLowerTriangular" | custom-call | tf_op jit(solution)/shard_map/triangular_solve/custom-call.8 | solution.py:34
  489.7 11.7 %cholesky.336 = f32[128,128]{1,0:T(8,128)S(1)} custom-call(f32[128,128]{1,0:T(8,128)S(1)} %fusion.19), custom_call_target="Cholesky" | custom-call | tf_op jit(solution)/shard_map/jit(cholesky)/cholesky | solution.py:33
  502.8 9.8 %custom-call.38 = f32[1,128,128]{1,2,0:T(8,128)S(1)} custom-call(f32[1,128,128]{2,1,0:T(8,128)S(1)} %fusion.12), custom_call_target="InvertDiagBlocksLowerTriangular" | custom-call | tf_op jit(solution)/shard_map/triangular_solve/custom-call.8 | solution.py:34
  516.6 11.9 %cholesky.347 = f32[128,128]{1,0:T(8,128)S(1)} custom-call(f32[128,128]{1,0:T(8,128)S(1)} %fusion.17), custom_call_target="Cholesky" | custom-call | tf_op jit(solution)/shard_map/jit(cholesky)/cholesky | solution.py:33
  529.8 9.8 %custom-call.39 = f32[1,128,128]{1,2,0:T(8,128)S(1)} custom-call(f32[1,128,128]{2,1,0:T(8,128)S(1)} %fusion.13), custom_call_target="InvertDiagBlocksLowerTriangular" | custom-call | tf_op jit(solution)/shard_map/triangular_solve/custom-call.8 | solution.py:34
  540.0 7.8 %fusion.8 = f32[128,4,1024]{2,0,1:T(8,128)} fusion(f32[4,1024,256]{2,1,0:T(8,128)} %bitcast.101, f32[512,128]{0,1:T(8,128)S(1)} %convolution_bitcast_fusion, s32[]{:T(128)S(6)} %select_n.11), kind=kOutput, calls=%fused_computation.20 | convolution fusion | flops 1610612736 | bytes 6422532 | tf_op jit(solution)/shard_map/dot_general | solution.py:65
  547.9 11.7 %reduce-scatter.2.cloned.1.call-done = f32[64,4,1024]{2,0,1:T(8,128)} async-done(((f32[128,4,1024]{2,0,1:T(8,128)}), f32[64,4,1024]{2,0,1:T(8,128)}) %reduce-scatter.2.cloned.1.call-update) | async-done | bytes 1048592 | tf_op jit(solution)/shard_map/reduce_scatter | solution.py:72
  (60 shorter events, 32.9 us)
Async XLA Ops:
  7.2 451.7 %copy-start = (f32[512,128]{1,0:T(8,128)S(1)}, f32[512,128]{1,0:T(8,128)}, u32[]{:S(2)}) copy-start(f32[512,128]{1,0:T(8,128)} %param.6) | copy-start | bytes 786436
  7.2 319.1 %all-reduce.4.cloned.1.call-start = ((), (), s32[]{:S(2)}) async-start(), calls=%async_computation.4 | async-start | bytes 2097152
  328.5 45.2 %all-to-all-start.1 = ((f32[512,1,512]{2,1,0:T(1,128)}), f32[512,1,512]{2,1,0:T(1,128)S(1)}, u32[]{:S(2)}, u32[]{:S(2)}) async-start(f32[512,1,512]{2,1,0:T(1,128)} %stack.2), calls=%async_computation.1 | async-start | bytes 2097152 | tf_op jit(solution)/shard_map/all_to_all | solution.py:13
  341.4 218.1 %reduce-scatter.2.cloned.1.call-start = ((), (), s32[]{:S(2)}) async-start(), calls=%async_computation.3 | async-start | bytes 3145728 | tf_op jit(solution)/shard_map/reduce_scatter | solution.py:72
  458.8 56.0 %copy-start.1 = (f32[512,512]{1,0:T(8,128)}, f32[512,512]{1,0:T(8,128)S(1)}, u32[]{:S(2)}) copy-start(f32[512,512]{1,0:T(8,128)S(1)} %select_select_fusion) | copy-start | bytes 3145732
Sparse Core Ops, SparseCore 0:
  51.8 274.4 all-reduce.3
  548.0 11.4 reduce-scatter.1
